TPU v7x, 256 devices: a whole 4x4x8 slice. The times are simulated.
256 devices in a mesh: expert: 16 (over x, y), edata: 16 (over z, core).
Axes of the slice: x: 4, y: 4, z: 8, core: 2. Of those that a mesh axis runs over, the one named last changes fastest.
Arguments:
- tokens: bfloat16 [1024, 7168], P(('expert', 'edata')), may hold values from -8 to 8
- routes: int32 [1024, 8], P(('expert', 'edata')), may hold values from 0 to 31, all different within a row; in each aligned block of 4 rows (0 to 3, 4 to 7, ...) at most 2 rows name the same one
- combine: bfloat16 [1024, 8], P(('expert', 'edata')), may hold values from 0.049804688 to 0.5
- w_gate: bfloat16 [32, 7168, 2048], P('expert', None, 'edata'), may hold values from -0.0625 to 0.0625
- w_up: bfloat16 [32, 7168, 2048], P('expert', None, 'edata')
- w_down: bfloat16 [32, 2048, 7168], P('expert', 'edata'), may hold values from -0.125 to 0.125
- past_amax: float32 [32], P('expert'), may hold values from 10 to 300
Outputs:
- layer_out: bfloat16 [1024, 7168], P(('expert', 'edata'))
- hidden_amax: float32 [32], P('expert')
Inputs may be any that keep to these rules, and one draw needn't show every extreme that they name: `routes`: each row names 8 different experts and every expert is named by some token. Among the 4 tokens of one device no expert is named more than 2 times, a bound that some block reaches.
All inputs are finite; a program needn't handle non-finite values.
Results may differ from a plain program's by a relative error of at most 0.018.
Values may be sent and summed in bfloat16 or wider, within the bound.
No kernel may reach another device: no remote copies, remote signals or barrier semaphores. Data moves between devices by JAX's collectives and lax.ppermute only.
A program may use at most 128 MiB of HBM per device.

v0:
```python
import jax
import jax.numpy as jnp
from jax import lax
from jax.sharding import PartitionSpec as P

quant_limit = 448.0


def route_tables(routes, combine, experts, capacity):
    tok_rows, fan_out = routes.shape
    flat_routes = routes.reshape(tok_rows * fan_out)
    expert_hits = (flat_routes[:, None] == jnp.arange(experts, dtype=jnp.int32)[None, :]).astype(
        jnp.int32
    )
    before = jnp.cumsum(expert_hits, axis=0) - expert_hits
    slot_rank = jnp.sum(expert_hits * before, axis=1)
    slot_index = flat_routes * capacity + slot_rank
    slot_table = (
        slot_index[:, None] == jnp.arange(experts * capacity, dtype=jnp.int32)[None, :]
    ).astype(jnp.float32)
    slot_table = slot_table.reshape(tok_rows, fan_out, experts * capacity)
    pick_table = jnp.sum(slot_table, axis=1)
    weights = jnp.sum(slot_table * combine.astype(jnp.float32)[:, :, None], axis=1)
    counts = jnp.sum(expert_hits, axis=0)
    return (pick_table, weights, counts)


def per_device(tokens, routes, combine, w_gate, w_up, w_down, past_amax):
    groups = lax.axis_size("expert")
    replicas = lax.axis_size("edata")
    local_experts = w_gate.shape[0]
    tok_rows = tokens.shape[0]
    fan_out = routes.shape[1]
    model_width = tokens.shape[1]
    hidden_units = w_gate.shape[2]
    experts = groups * local_experts
    capacity = min(tok_rows, max(2, 2 * tok_rows * fan_out // experts))
    group_rows = groups * local_experts * capacity
    pick_table, weights, counts = route_tables(routes, combine, experts, capacity)
    outgoing = jnp.dot(
        pick_table.T.astype(jnp.bfloat16), tokens, preferred_element_type=jnp.float32
    )
    outgoing = outgoing.astype(jnp.bfloat16).reshape(groups, local_experts * capacity, model_width)
    arrived, arrived_counts = (
        lax.all_to_all(outgoing, "expert", split_axis=0, concat_axis=0, tiled=True),
        lax.all_to_all(
            counts.reshape(groups, local_experts), "expert", split_axis=0, concat_axis=0, tiled=True
        ),
    )
    rows_all, counts_all = (
        lax.all_gather(arrived[None], "edata", axis=0, tiled=True),
        lax.all_gather(arrived_counts[None], "edata", axis=0, tiled=True),
    )
    slot_rows = rows_all.reshape(replicas, groups, local_experts, capacity, model_width)
    occupied = jnp.arange(capacity, dtype=jnp.int32)[None, None, None, :] < counts_all[..., None]
    quant_gain = quant_limit / past_amax
    dequant = past_amax / quant_limit
    gate_proj = jnp.einsum(
        "abjcx,jxf->abjcf", slot_rows, w_gate, preferred_element_type=jnp.float32
    )
    up_proj = jnp.einsum("abjcx,jxf->abjcf", slot_rows, w_up, preferred_element_type=jnp.float32)
    hidden = jax.nn.silu(gate_proj) * up_proj
    local_max = jnp.max(jnp.where(occupied[..., None], jnp.abs(hidden), 0.0), axis=(0, 1, 3, 4))
    quantized = jnp.clip(
        hidden * quant_gain[None, None, :, None, None], -quant_limit, quant_limit
    ).astype(jnp.bfloat16)
    quant_rows = quantized.reshape(replicas * group_rows, hidden_units)
    hidden_amax = lax.pmax(local_max, "edata")
    quant_piece = quant_rows
    quant_piece = quant_piece.reshape(
        lax.axis_size("edata") * group_rows // (local_experts * capacity),
        local_experts,
        capacity,
        hidden_units,
    )
    down_proj = jnp.einsum(
        "njcf,jfx->njcx", quant_piece, w_down, preferred_element_type=jnp.float32
    )
    reduced = lax.psum_scatter(
        (down_proj * dequant[None, :, None, None])
        .reshape(lax.axis_size("edata") * group_rows, model_width)
        .astype(jnp.bfloat16),
        "edata",
        scatter_dimension=0,
        tiled=True,
    ).astype(jnp.float32)
    back_rows = lax.all_to_all(
        reduced.reshape(groups, local_experts * capacity, model_width).astype(jnp.bfloat16),
        "expert",
        split_axis=0,
        concat_axis=0,
        tiled=True,
    ).astype(jnp.float32)
    layer_out = jnp.dot(
        weights,
        back_rows.reshape(experts * capacity, model_width),
        precision=lax.Precision.HIGHEST,
        preferred_element_type=jnp.float32,
    )
    return (layer_out.astype(jnp.bfloat16), hidden_amax)


def solution(mesh):
    return jax.shard_map(
        per_device,
        mesh=mesh,
        in_specs=(
            P(("expert", "edata"), None),
            P(("expert", "edata"), None),
            P(("expert", "edata"), None),
            P("expert", None, "edata"),
            P("expert", None, "edata"),
            P("expert", "edata", None),
            P("expert"),
        ),
        out_specs=(P(("expert", "edata"), None), P("expert")),
        check_vma=False,
    )
```

profile of v0, /device:TPU:2, one launch (start us, length us, event | category | flops | bytes accessed | tf_op | source)
XLA Modules:
  0.0 335.1 jit_solution(13462882014984039746)
XLA Ops:
  7.2 0.0 copy-start
  7.2 0.0 all-gather.4.cloned.1.call-start
  7.2 0.8 eq.29
  8.0 0.7 convert_element_type.39
  8.7 0.1 fusion.23
  8.7 0.1 reduce_window_sum.11
  8.8 0.2 fusion.24
  9.0 0.1 reduce_sum.39
  9.1 0.7 multiply_add_fusion
  9.8 0.1 convert_reduce_fusion
  9.9 0.0 copy-done
  9.9 0.5 convolution_convert_fusion
  10.3 0.3 reshape.48
  10.7 20.9 %all_to_all.19 = bf16[16,4,7168]{2,1,0:T(4,128)(2,1)S(1)} all-to-all(bf16[16,4,7168]{2,1,0:T(4,128)(2,1)S(1)} %reshape.48), channel_id=1, replica_groups=mesh['expert'=16,'edata'=16] {'expert'}, dimensions={0} | all-to-all | bytes 1835008 | tf_op jit(solution)/shard_map/all_to_all | solution.py:45
  31.6 1.2 copy.30
  32.8 0.0 all-gather.4.cloned.1.call-update
  32.8 0.7 all_to_all.14
  33.5 5.6 %all-to-all-start.2 = ((s32[16,1,2]{2,1,0:T(1,128)}), s32[16,1,2]{2,1,0:T(1,128)S(1)}, u32[]{:S(2)}, u32[]{:S(2)}) async-start(s32[16,1,2]{2,1,0:T(1,128)} %bitcast.11), calls=%async_computation.3 | async-start | bytes 16384 | tf_op jit(solution)/shard_map/all_to_all | solution.py:46
  39.1 0.0 reduce-scatter.2.cloned.1.call-start
  39.1 0.7 broadcast_divide_fusion
  39.8 5.4 %all-to-all-done.2 = s32[16,1,2]{2,1,0:T(1,128)S(1)} async-done(((s32[16,1,2]{2,1,0:T(1,128)}), s32[16,1,2]{2,1,0:T(1,128)S(1)}, u32[]{:S(2)}, u32[]{:S(2)}) %all-to-all-start.2) | async-done | bytes 160 | tf_op jit(solution)/shard_map/all_to_all | solution.py:46
  45.2 21.5 %all-gather.1 = s32[256,1,2]{2,1,0:T(1,128)S(1)} all-gather(s32[16,1,2]{2,1,0:T(1,128)S(1)} %all-to-all-done.2), channel_id=3, replica_groups=mesh['expert'=16,'edata'=16] {'edata'}, dimensions={0}, use_global_device_ids=true | all-gather | bytes 2176 | tf_op jit(solution)/shard_map/all_gather | solution.py:52
  66.7 0.1 copy.36
  66.9 53.3 %all-gather.4.cloned.1.call-done = bf16[256,4,7168]{2,0,1:T(8,128)(2,1)} async-done(((bf16[16,4,7168]{2,0,1:T(8,128)(2,1)}), bf16[256,4,7168]{2,0,1:T(8,128)(2,1)}) %all-gather.4.cloned.1.call-update) | async-done | bytes 14680080 | tf_op jit(solution)/shard_map/all_gather | solution.py:51
  120.2 8.5 %fusion.8 = f32[16,16,2,2,128]{4,1,3,0,2:T(8,128)S(1)} fusion(bf16[2,7168,128]{2,1,0:T(8,128)(2,1)} %param.10, bf16[16,16,2,2,7168]{4,1,0,3,2:T(8,128)(2,1)} %bitcast.42), kind=kOutput, calls=%fused_computation.11 | convolution fusion | flops 1879048192 | bytes 18874368 | tf_op jit(solution)/shard_map/abjcx,jxf->abjcf/dot_general | solution.py:58
  128.7 0.0 copy-start.2
  128.7 10.5 %select_reduce_fusion = (f32[2]{0:T(128)S(1)}, bf16[16,16,2,2,128]{4,1,3,0,2:T(8,128)(2,1)S(1)}) fusion(pred[16,16,2,2]{1,3,0,2:T(4,128)(4,1)S(1)} %iota_compare_fusion, f32[2]{0:T(128)S(1)} %get-tuple-element.8, bf16[2,7168,128]{2,1,0:T(8,128)(2,1)} %param.11, bf16[16,16,2,2,7168]{4,1,0,3,2:T(8,128)(2,1)} %bitcast.43, f32[16,16,2,2,128]{4,1,3,0,2:T(8,128)S(1)} %fusion.8), kind=kOutput, calls=%fused_computation.14 | convolution fusion | flops 1880489984 | bytes 19137552 | tf_op jit(solution)/shard_map/abjcx,jxf->abjcf/dot_general | solution.py:61
  139.2 0.0 copy-done.2
  139.2 7.3 %fusion.4 = bf16[256,2,2,7168]{3,0,2,1:T(8,128)(2,1)} fusion(f32[2]{0:T(128)S(1)} %get-tuple-element.9, bf16[256,2,2,128]{3,0,2,1:T(8,128)(2,1)S(1)} %bitcast.40, bf16[2,128,7168]{2,1,0:T(8,128)(2,1)S(1)} %copy-done.2), kind=kOutput, calls=%fused_computation.5 | convolution fusion | flops 1893728256 | bytes 18612232 | tf_op jit(solution)/shard_map/njcf,jfx->njcx/dot_general | solution.py:76
  146.5 27.5 %copy.34 = bf16[256,2,2,7168]{3,2,1,0:T(2,128)(2,1)} copy(bf16[256,2,2,7168]{3,0,2,1:T(8,128)(2,1)} %fusion.4) | data formatting | bytes 29360128 | tf_op jit(solution)/shard_map/convert_element_type | solution.py:82
  174.0 0.0 copy-start.1
  174.0 29.3 %convert_element_type.46 = bf16[1024,7168]{1,0:T(8,128)(2,1)} reshape(bf16[256,2,2,7168]{3,2,1,0:T(2,128)(2,1)} %copy.34) | data formatting | bytes 29360128 | tf_op jit(solution)/shard_map/convert_element_type | solution.py:82
  203.3 0.0 reduce-scatter.2.cloned.1.call-update
  203.3 88.7 %reduce-scatter.2.cloned.1.call-done = bf16[64,7168]{1,0:T(8,128)(2,1)} async-done(((bf16[1024,7168]{1,0:T(8,128)(2,1)}), bf16[64,7168]{1,0:T(8,128)(2,1)}) %reduce-scatter.2.cloned.1.call-update) | async-done | bytes 917520 | tf_op jit(solution)/shard_map/reduce_scatter | solution.py:79
  292.0 2.5 convert_element_type.47
  294.5 7.3 %all-to-all-start.1 = ((bf16[16,4,7168]{2,1,0:T(4,128)(2,1)}), bf16[16,4,7168]{2,1,0:T(4,128)(2,1)S(1)}, u32[]{:S(2)}, u32[]{:S(2)}) async-start(bf16[16,4,7168]{2,1,0:T(4,128)(2,1)} %convert_element_type.47), calls=%async_computation.2 | async-start | bytes 1835008 | tf_op jit(solution)/shard_map/all_to_all | solution.py:87
  301.8 25.2 %pmax.7 = f32[2]{0:T(128)} all-reduce(f32[2]{0:T(128)S(1)} %get-tuple-element.6), channel_id=1, replica_groups=mesh['expert'=16,'edata'=16] {'edata'}, use_global_device_ids=true, to_apply=%region_7.8 | all-reduce | flops 2 | bytes 16 | tf_op jit(solution)/shard_map/pmax | solution.py:68
  327.0 0.0 all-to-all-done.1
  327.0 0.2 reshape.50
  327.2 1.1 convolution_convert_fusion.1
  328.3 0.0 copy-done.1
  (2 shorter events, 0.1 us)
Async XLA Ops:
  7.2 2.7 copy-start
  7.2 113.0 %all-gather.4.cloned.1.call-start = ((), (), s32[]{:S(2)}) async-start(), calls=%async_computation.5 | async-start | bytes 15597568 | tf_op jit(solution)/shard_map/all_gather | solution.py:51
  33.5 11.8 %all-to-all-start.2 = ((s32[16,1,2]{2,1,0:T(1,128)}), s32[16,1,2]{2,1,0:T(1,128)S(1)}, u32[]{:S(2)}, u32[]{:S(2)}) async-start(s32[16,1,2]{2,1,0:T(1,128)} %bitcast.11), calls=%async_computation.3 | async-start | bytes 16384 | tf_op jit(solution)/shard_map/all_to_all | solution.py:46
  39.1 252.9 %reduce-scatter.2.cloned.1.call-start = ((), (), s32[]{:S(2)}) async-start(), calls=%async_computation.4 | async-start | bytes 15597568 | tf_op jit(solution)/shard_map/reduce_scatter | solution.py:79
  128.7 10.5 %copy-start.2 = (bf16[2,128,7168]{2,1,0:T(8,128)(2,1)S(1)}, bf16[2,128,7168]{2,1,0:T(8,128)(2,1)}, u32[]{:S(2)}) copy-start(bf16[2,128,7168]{2,1,0:T(8,128)(2,1)} %param.12) | copy-start | bytes 11010052
  174.0 154.3 %copy-start.1 = (bf16[4,7168]{1,0:T(4,128)(2,1)S(1)}, bf16[4,7168]{1,0:T(4,128)(2,1)}, u32[]{:S(2)}) copy-start(bf16[4,7168]{1,0:T(4,128)(2,1)} %param.7) | copy-start | bytes 172036
  294.5 32.4 %all-to-all-start.1 = ((bf16[16,4,7168]{2,1,0:T(4,128)(2,1)}), bf16[16,4,7168]{2,1,0:T(4,128)(2,1)S(1)}, u32[]{:S(2)}, u32[]{:S(2)}) async-start(bf16[16,4,7168]{2,1,0:T(4,128)(2,1)} %convert_element_type.47), calls=%async_computation.2 | async-start | bytes 1835008 | tf_op jit(solution)/shard_map/all_to_all | solution.py:87
Sparse Core Ops, SparseCore 0:
  32.9 87.2 all-gather.3
  203.4 88.4 reduce-scatter.1
where the time goes:
time: 336 us; the launch traced here: 335 us
  waiting for transfers between devices  147 us (44%)
  blocking collectives  67.6 us (20%)
  local copies, waits for them, and re-layouts  62.8 us (19%)
  matrix products  27.8 us (8%)
  between operations  14.1 us (4%)
  starting transfers between devices  13 us (4%)
    reduce_scatter x1, waiting for transfers between devices, per_device(): lax.psum_scatter((down_proj * dequant[None, :, None, None]).reshape(lax.a...  88.7 us
    convert_element_type x2, local copies, waits for them, and re-layouts, per_device(): reduced = lax.psum_scatter((down_proj * dequant[None, :, None, None]).res...  56.8 us
    all_gather x1, waiting for transfers between devices, per_device(): lax.all_gather(arrived[None], 'edata', axis=0, tiled=True)  53.3 us
    pmax x1, blocking collectives, per_device(): hidden_amax = lax.pmax(local_max, 'edata')  25.2 us
    all_gather x1, blocking collectives, per_device(): lax.all_gather(arrived_counts[None], 'edata', axis=0, tiled=True)  21.5 us
    all_to_all x1, blocking collectives, per_device(): lax.all_to_all(outgoing, 'expert', split_axis=0, concat_axis=0, tiled=True)  20.9 us
    dot_general x1, matrix products, per_device(): jnp.einsum('abjcx,jxf->abjcf', slot_rows, w_up, preferred_element_type=jn...  10.5 us
    dot_general x1, matrix products, per_device(): jnp.einsum('abjcx,jxf->abjcf', slot_rows, w_gate, preferred_element_type=...  8.48 us
  transfers between devices with their start and end apart: 4, of which 3 were waited for; matrix products, arithmetic and copies ran while one was open for 0% of the time, Pallas kernels for 0%

commit v1 on v0

v1 whole, which is shorter than its diff:
```python
import jax
import jax.numpy as jnp
from jax import lax
from jax.sharding import PartitionSpec as P

quant_limit = 448.0
lane = 128


def per_device(tokens, routes, combine, w_gate, w_up, w_down, past_amax):
    groups = lax.axis_size("expert")
    members = lax.axis_size("edata")
    local_experts, model_width, hidden_units = w_gate.shape
    rows = tokens.shape[0]
    half = model_width // 2
    fan = local_experts * hidden_units
    experts = groups * local_experts
    core = lax.axis_index("edata") % 2
    group = lax.axis_index("expert")
    swap = [(i, i ^ 1) for i in range(members)]

    lanes = jnp.arange(lane, dtype=jnp.int32)
    hits = routes[:, :, None] == lanes[None, None, :]
    weights = jnp.sum(jnp.where(hits, combine.astype(jnp.float32)[:, :, None], 0.0), axis=1)
    weights = weights.astype(jnp.bfloat16)

    pieces = jnp.stack(
        [
            jnp.concatenate([tokens[:, :half], weights], axis=1),
            jnp.concatenate([tokens[:, half:], weights], axis=1),
        ]
    )
    outgoing = jnp.broadcast_to(
        pieces[None], (members // 2, 2, rows, half + lane)
    ).reshape(members, rows, half + lane)
    line = lax.all_to_all(outgoing, "edata", split_axis=0, concat_axis=0, tiled=True)
    line = line.reshape(members * rows, half + lane)
    line, w_gate, w_up, w_down = lax.optimization_barrier((line, w_gate, w_up, w_down))
    everyone = lax.all_gather(line, "expert", axis=0, tiled=True)

    def mine_and_other(w, axis):
        keep = lax.dynamic_slice_in_dim(w, core * half, half, axis=axis)
        give = lax.dynamic_slice_in_dim(w, (1 - core) * half, half, axis=axis)
        return keep, lax.ppermute(give, "edata", swap)

    gate_keep, gate_got = mine_and_other(w_gate, 1)
    up_keep, up_got = mine_and_other(w_up, 1)
    down_keep, down_got = mine_and_other(w_down, 2)

    def side(w):
        return [w[j] for j in range(local_experts)]

    w_other = jnp.concatenate(side(gate_got) + side(up_got), axis=1)
    w_own_gate = jnp.concatenate(side(gate_keep), axis=1)
    w_own_up = jnp.concatenate(side(up_keep), axis=1)
    w_out = jnp.concatenate(
        [down_keep.reshape(fan, half), down_got.reshape(fan, half)], axis=0
    )

    everyone, w_other, w_own_gate, w_own_up, w_out = lax.optimization_barrier(
        (everyone, w_other, w_own_gate, w_own_up, w_out)
    )
    features = everyone[:, :half]

    unit_expert = jnp.arange(fan, dtype=jnp.int32) // hidden_units
    spread = (lanes[:, None] == group * local_experts + unit_expert[None, :]).astype(jnp.bfloat16)
    quant_gain = jnp.repeat(quant_limit / past_amax, hidden_units)
    dequant = jnp.repeat(past_amax / quant_limit, hidden_units)

    other = jnp.dot(features, w_other, preferred_element_type=jnp.float32)
    got = lax.ppermute(other, "edata", swap)
    weight = jnp.dot(everyone[:, half:], spread, preferred_element_type=jnp.float32)
    own_gate = jnp.dot(features, w_own_gate, preferred_element_type=jnp.float32)
    own_up = jnp.dot(features, w_own_up, preferred_element_type=jnp.float32)
    gate_proj = own_gate + got[:, :fan]
    up_proj = own_up + got[:, fan:]
    hidden = jax.nn.silu(gate_proj) * up_proj
    peaks = jnp.max(jnp.where(weight > 0.0, jnp.abs(hidden), 0.0), axis=0)
    peaks = jnp.max(peaks.reshape(local_experts, hidden_units), axis=1)
    clipped = jnp.clip(hidden * quant_gain[None, :], -quant_limit, quant_limit)
    scaled = (clipped * (weight * dequant[None, :])).astype(jnp.bfloat16)
    both = jnp.concatenate([scaled, lax.ppermute(scaled, "edata", swap)], axis=1)
    down = jnp.dot(both, w_out, preferred_element_type=jnp.float32).astype(jnp.bfloat16)
    reduced = lax.psum_scatter(down, "expert", scatter_dimension=0, tiled=True)
    hidden_amax = lax.pmax(peaks, "edata")
    reduced, hidden_amax = lax.optimization_barrier((reduced, hidden_amax))
    reduced = reduced.reshape(members, rows, half)
    back = lax.all_to_all(reduced, "edata", split_axis=0, concat_axis=0, tiled=True)
    total = jnp.sum(back.reshape(members // 2, 2, rows, half).astype(jnp.float32), axis=0)
    layer_out = jnp.concatenate([total[0], total[1]], axis=1)
    return (layer_out.astype(jnp.bfloat16), hidden_amax)


def solution(mesh):
    return jax.shard_map(
        per_device,
        mesh=mesh,
        in_specs=(
            P(("expert", "edata"), None),
            P(("expert", "edata"), None),
            P(("expert", "edata"), None),
            P("expert", None, "edata"),
            P("expert", None, "edata"),
            P("expert", "edata", None),
            P("expert"),
        ),
        out_specs=(P(("expert", "edata"), None), P("expert")),
        check_vma=False,
    )
```

time: 336 us -> 255 us (0.76)
  local copies, waits for them, and re-layouts: 62.8 us -> 6.71 us
  waiting for transfers between devices: 147 us -> 120 us
  starting transfers between devices: 13 us -> 4.37 us
  other arithmetic: 2.48 us -> 8.65 us
  blocking collectives: 67.6 us -> 72.8 us
    convert_element_type x4 -> x0, local copies, waits for them, and re-layouts: 59.3 us -> none  [the longest x2 56.8 us: per_device(): reduced = lax.psum_scatter((down_proj * dequant[None, :, None, None]).res...]
    reduce_scatter x1, waiting for transfers between devices: 88.7 us -> 60.6 us  [per_device(): reduced = lax.psum_scatter(down, 'expert', scatter_dimension=0, tiled=True)]
    all_to_all x1 -> x2, blocking collectives: 20.9 us -> 45.1 us  [the longest x1 23.4 us: per_device(): lax.all_to_all(outgoing, 'edata', split_axis=0, concat_axis=0, tiled=True)]
    all_gather x1 -> x0, blocking collectives: 21.5 us -> none  [per_device(): lax.all_gather(arrived_counts[None], 'edata', axis=0, tiled=True)]
    all_to_all x2 -> x0, starting transfers between devices: 12.9 us -> none  [the longest x1 7.27 us: per_device(): lax.all_to_all(reduced.reshape(groups, local_experts * capacity, model_wi...]
    concatenate x0 -> x5, other arithmetic: none -> 6.61 us  [the longest x1 2.16 us: per_device(): jnp.concatenate([down_keep.reshape(fan, half), down_got.reshape(fan, half...]
    all_to_all x2 -> x0, waiting for transfers between devices: 5.44 us -> none  [the longest x1 5.44 us: per_device(): lax.all_to_all(counts.reshape(groups, local_experts), 'expert', split_axi...]
    ppermute x0 -> x5, starting transfers between devices: none -> 4.29 us  [the longest x3 3.69 us: mine_and_other(): return (keep, lax.ppermute(give, 'edata', swap))]
  transfers between devices with their start and end apart: 4 -> 7, of which waited for: 3 -> 4; matrix products, arithmetic and copies ran while one was open for 0% -> 7% of each run, Pallas kernels for 0% -> 0%
where the time goes in v1:
time: 255 us; the launch traced here: 252 us
  waiting for transfers between devices  120 us (47%)
  blocking collectives  72.8 us (29%)
  matrix products  25 us (10%)
  between operations  14.2 us (6%)
  other arithmetic  8.65 us (3%)
  local copies, waits for them, and re-layouts  6.71 us (3%)
  starting transfers between devices  4.37 us (2%)
    reduce_scatter x1, waiting for transfers between devices, per_device(): reduced = lax.psum_scatter(down, 'expert', scatter_dimension=0, tiled=True)  60.6 us
    all_gather x1, waiting for transfers between devices, per_device(): everyone = lax.all_gather(line, 'expert', axis=0, tiled=True)  55.8 us
    pmax x1, blocking collectives, per_device(): hidden_amax = lax.pmax(peaks, 'edata')  27.7 us
    all_to_all x1, blocking collectives, per_device(): lax.all_to_all(outgoing, 'edata', split_axis=0, concat_axis=0, tiled=True)  23.4 us
    all_to_all x1, blocking collectives, per_device(): lax.all_to_all(reduced, 'edata', split_axis=0, concat_axis=0, tiled=True)  21.7 us
    dot_general x1, matrix products, per_device(): other = jnp.dot(features, w_other, preferred_element_type=jnp.float32)  9.38 us
    dot_general x1, matrix products, per_device(): jnp.dot(both, w_out, preferred_element_type=jnp.float32)  5.97 us
    dot_general x1, matrix products, per_device(): own_gate = jnp.dot(features, w_own_gate, preferred_element_type=jnp.float32)  5.29 us
  transfers between devices with their start and end apart: 7, of which 4 were waited for; matrix products, arithmetic and copies ran while one was open for 7% of the time, Pallas kernels for 0%

profile of v1, /device:TPU:2, one launch (start us, length us, event | category | flops | bytes accessed | tf_op | source)
XLA Modules:
  0.0 251.8 jit_solution(4758817106021248310)
XLA Ops:
  7.2 0.0 all-gather.2.cloned.1.call-start
  7.2 0.8 fusion.18
  8.0 0.7 convert_element_type.20
  8.7 0.8 select_reduce_fusion.1
  9.5 0.1 broadcast_in_dim.33
  9.7 23.4 %all_to_all.10 = bf16[16,4,3712]{2,1,0:T(4,128)(2,1)S(1)} all-to-all(bf16[16,4,3712]{2,1,0:T(4,128)(2,1)S(1)} %bitcast.39), channel_id=1, replica_groups=mesh['expert'=16,'edata'=16] {'edata'}, dimensions={0} | all-to-all | bytes 950272 | tf_op jit(solution)/shard_map/all_to_all | solution.py:36
  33.1 0.9 reshape.46
  34.0 0.0 all-gather.2.cloned.1.call-update
  34.0 0.0 reduce-scatter.2.cloned.1.call-start
  34.1 0.0 copy-start.2
  34.1 2.4 constant_dynamic-slice_fusion.1
  36.6 0.0 copy-start.1
  36.6 1.6 collective-permute-start.2
  38.2 0.1 constant_dynamic-slice_fusion.3
  38.3 0.7 collective-permute-start
  39.0 0.1 constant_dynamic-slice_fusion.2
  39.1 1.4 collective-permute-start.1
  40.5 0.2 dynamic-slice_bitcast_fusion.1
  40.8 0.2 pad_maximum_fusion.2
  41.0 1.5 pad_maximum_fusion.3
  42.4 0.0 collective-permute-done.2
  42.4 2.2 pad_maximum_fusion.1
  44.6 0.0 collective-permute-done
  44.6 0.1 slice_bitcast_fusion.3
  44.7 2.1 collective-permute-done.1
  46.9 0.1 slice_bitcast_fusion.1
  47.0 2.1 pad_maximum_fusion
  49.1 55.8 %all-gather.2.cloned.1.call-done = bf16[1024,3712]{1,0:T(8,128)(2,1)} async-done(((bf16[64,3712]{1,0:T(8,128)(2,1)}), bf16[1024,3712]{1,0:T(8,128)(2,1)}) %all-gather.2.cloned.1.call-update) | async-done | bytes 7602192 | tf_op jit(solution)/shard_map/all_gather | solution.py:39
  104.9 9.4 %fusion.2 = f32[1024,512]{1,0:T(8,128)} fusion(bf16[3584,512]{1,0:T(8,128)(2,1)} %pad_maximum_fusion, bf16[1024,3712]{1,0:T(8,128)(2,1)} %all-gather.2.cloned.1.call-done), kind=kOutput, calls=%fused_computation.3 | convolution fusion | flops 3758096384 | bytes 13107200 | tf_op jit(solution)/shard_map/dot_general | solution.py:70
  114.3 0.0 collective-permute-start.3
  114.3 0.1 broadcast_bitcast_fusion
  114.4 5.3 %fusion.4 = f32[1024,256]{1,0:T(8,128)S(1)} fusion(bf16[3584,256]{1,0:T(8,128)(2,1)S(1)} %pad_maximum_fusion.2, bf16[1024,3712]{1,0:T(8,128)(2,1)} %all-gather.2.cloned.1.call-done), kind=kOutput, calls=%fused_computation.5 | convolution fusion | flops 1879048192 | bytes 10223616 | tf_op jit(solution)/shard_map/dot_general | solution.py:73
  119.7 0.5 copy-done.4
  120.2 2.1 fusion
  122.3 0.0 collective-permute-done.3
  122.3 2.3 select_reduce_fusion
  124.6 0.2 multiply_convert_fusion
  124.8 0.6 collective-permute-start.4
  125.4 1.5 collective-permute-done.4
  126.9 6.0 %convolution_convert_fusion = bf16[1024,3584]{1,0:T(8,128)(2,1)} fusion(bf16[512,3584]{1,0:T(8,128)(2,1)S(1)} %copy-done, bf16[1024,256]{1,0:T(8,128)(2,1)S(1)} %collective-permute-done.4, bf16[1024,256]{1,0:T(8,128)(2,1)S(1)} %multiply_convert_fusion), kind=kOutput, calls=%fused_computation | convolution fusion | flops 3763863552 | bytes 12058624 | tf_op jit(solution)/shard_map/dot_general | solution.py:83
  132.9 0.0 reduce-scatter.2.cloned.1.call-update
  132.9 0.1 bitcast_reduce_fusion
  133.0 27.7 %pmax.7 = f32[2]{0:T(128)} all-reduce(f32[2]{0:T(128)S(1)} %bitcast_reduce_fusion), channel_id=1, replica_groups=mesh['expert'=16,'edata'=16] {'edata'}, use_global_device_ids=true, to_apply=%region_4.5 | all-reduce | flops 2 | bytes 16 | tf_op jit(solution)/shard_map/pmax | solution.py:85
  160.7 60.6 %reduce-scatter.2.cloned.1.call-done = bf16[64,3584]{1,0:T(8,128)(2,1)} async-done(((bf16[1024,3584]{1,0:T(8,128)(2,1)}), bf16[64,3584]{1,0:T(8,128)(2,1)}) %reduce-scatter.2.cloned.1.call-update) | async-done | bytes 458768 | tf_op jit(solution)/shard_map/reduce_scatter | solution.py:84
  221.3 1.1 reshape.50
  222.4 21.7 %all_to_all.11 = bf16[16,4,3584]{2,1,0:T(4,128)(2,1)S(1)} all-to-all(bf16[16,4,3584]{2,1,0:T(4,128)(2,1)S(1)} %reshape.50), channel_id=1, replica_groups=mesh['expert'=16,'edata'=16] {'edata'}, dimensions={0} | all-to-all | bytes 917504 | tf_op jit(solution)/shard_map/all_to_all | solution.py:88
  244.1 0.2 reduce
  244.3 0.7 pad_maximum_fusion.5
  (14 shorter events, 0.1 us)
Async XLA Ops:
  7.2 97.8 %all-gather.2.cloned.1.call-start = ((), (), s32[]{:S(2)}) async-start(), calls=%async_computation.3 | async-start | bytes 8077312 | tf_op jit(solution)/shard_map/all_gather | solution.py:39
  34.0 187.3 %reduce-scatter.2.cloned.1.call-start = ((), (), s32[]{:S(2)}) async-start(), calls=%async_computation.4 | async-start | bytes 7798784 | tf_op jit(solution)/shard_map/reduce_scatter | solution.py:84
  34.1 4.1 %copy-start.2 = (bf16[2,7168,128]{2,1,0:T(8,128)(2,1)S(1)}, bf16[2,7168,128]{2,1,0:T(8,128)(2,1)}, u32[]{:S(2)}) copy-start(bf16[2,7168,128]{2,1,0:T(8,128)(2,1)} %param.10) | copy-start | bytes 11010052
  36.6 2.4 copy-start.1
  36.6 5.9 %collective-permute-start.2 = (bf16[2,128,3584]{2,1,0:T(8,128)(2,1)S(1)}, bf16[2,128,3584]{2,1,0:T(8,128)(2,1)S(1)}, u32[]{:S(2)}, u32[]{:S(2)}) collective-permute-start(bf16[2,128,3584]{2,1,0:T(8,128)(2,1)S(1)} %get-tuple-element.27), channel_id=1, source_target_pairs={{0,1},{1,0},{2,3},{3,2},{4,5},{5,4},{6,7},{7,6},{8,9},{9,8},{10,11... | collective-permute-start | bytes 5505032 | tf_op jit(solution)/shard_map/ppermute | solution.py:44
  38.3 6.3 %collective-permute-start = (bf16[2,3584,128]{2,1,0:T(8,128)(2,1)S(1)}, bf16[2,3584,128]{2,1,0:T(8,128)(2,1)S(1)}, u32[]{:S(2)}, u32[]{:S(2)}) collective-permute-start(bf16[2,3584,128]{2,1,0:T(8,128)(2,1)S(1)} %constant_dynamic-slice_fusion.3), channel_id=1, source_target_pairs={{0,1},{1,0},{2,3},{3,2},{4,5},{5,4},{6,7},{7,6},{8,9},{9,8},{10,11... | collective-permute-start | bytes 5505032 | tf_op jit(solution)/shard_map/ppermute | solution.py:44
  39.1 7.7 %collective-permute-start.1 = (bf16[2,3584,128]{2,1,0:T(8,128)(2,1)S(1)}, bf16[2,3584,128]{2,1,0:T(8,128)(2,1)S(1)}, u32[]{:S(2)}, u32[]{:S(2)}) collective-permute-start(bf16[2,3584,128]{2,1,0:T(8,128)(2,1)S(1)} %constant_dynamic-slice_fusion.2), channel_id=1, source_target_pairs={{0,1},{1,0},{2,3},{3,2},{4,5},{5,4},{6,7},{7,6},{8,9},{9,8},{10,11... | collective-permute-start | bytes 5505032 | tf_op jit(solution)/shard_map/ppermute | solution.py:44
  49.1 65.2 %copy-start.5 = (f32[2]{0:T(128)S(1)}, f32[2]{0:T(128)}, u32[]{:S(2)}) copy-start(f32[2]{0:T(128)} %param.13) | copy-start | bytes 28
  114.3 8.0 %collective-permute-start.3 = (f32[1024,512]{1,0:T(8,128)}, f32[1024,512]{1,0:T(8,128)}, u32[]{:S(2)}, u32[]{:S(2)}) collective-permute-start(f32[1024,512]{1,0:T(8,128)} %fusion.2), channel_id=1, source_target_pairs={{0,1},{1,0},{2,3},{3,2},{4,5},{5,4},{6,7},{7,6},{8,9},{9,8},{10,11... | collective-permute-start | bytes 6291464 | tf_op jit(solution)/shard_map/ppermute | solution.py:71
  114.4 5.3 %copy-start.3 = (bf16[3584,256]{1,0:T(8,128)(2,1)S(1)}, bf16[3584,256]{1,0:T(8,128)(2,1)}, u32[]{:S(2)}) copy-start(bf16[3584,256]{1,0:T(8,128)(2,1)} %pad_maximum_fusion.3) | copy-start | bytes 5505028
  114.4 5.8 %copy-start.4 = (bf16[1024,3712]{1,0:T(8,128)(2,1)S(1)}, bf16[1024,3712]{1,0:T(8,128)(2,1)}, u32[]{:S(2)}) copy-start(bf16[1024,3712]{1,0:T(8,128)(2,1)} %all-gather.2.cloned.1.call-done) | copy-start | bytes 22806532
  122.3 4.6 %copy-start = (bf16[512,3584]{1,0:T(8,128)(2,1)S(1)}, bf16[512,3584]{1,0:T(8,128)(2,1)}, u32[]{:S(2)}) copy-start(bf16[512,3584]{1,0:T(8,128)(2,1)} %pad_maximum_fusion.1) | copy-start | bytes 11010052
  124.8 2.1 collective-permute-start.4
Sparse Core Ops, SparseCore 0:
  34.2 70.7 all-gather.1
  133.0 88.2 reduce-scatter.1
